TPU v7x, 32 devices: a whole 2x2x4 slice. The times are simulated.
32 devices in a mesh: groups: 2 (over y), owners: 4 (over z), section: 2 (over x), rep: 2 (over core).
Axes of the slice: x: 2, y: 2, z: 4, core: 2. Of those that a mesh axis runs over, the one named last changes fastest.
Arguments:
- inputs: bfloat16 [2, 4096, 512], P('section', 'owners', ('groups', 'rep')), parts along dimension 2, may hold values from -6 to 6
- weight_first: bfloat16 [2, 32, 2048, 128], P('section', ('owners', 'rep')), may hold values from -0.1875 to 0.1875
- weight_second: bfloat16 [2, 32, 1024, 128], P('section', ('owners', 'rep')), may hold values from -0.25 to 0.25
- bias_first: float32 [2, 4096], P('section', 'owners'), may hold values from -1.5 to 1.5
- bias_second: float32 [2, 4096], P('section', 'owners'), may hold values from -1.5 to 1.5
- links_first: int32 [2, 32, 16], P('section', 'owners'), may hold values from 0 to 15, as said below
- links_second: int32 [2, 32, 8], P('section', 'owners'), may hold values from 0 to 7, as said below
Outputs:
- final_activity: bfloat16 [2, 4096, 512], P('section', 'owners', ('groups', 'rep')), parts along dimension 2
There are 2 independent parts, one for each index of `groups`. A program takes and returns all parts, laid end to end along the dimension named above; an argument that names none is the same for every part. Nothing has to cross between parts.
Inputs may be any that keep to these rules, and one draw needn't show every extreme that they name: `links_first`: in every row of every section the 16 entries are distinct. `links_second`: in every row of every section the 8 entries are distinct.
All inputs are finite; a program needn't handle non-finite values.
Results may differ from a plain program's by a relative error of at most 0.014.
Values may be sent and summed in bfloat16 or wider, within the bound.
A program may use at most 64 MiB of HBM per device.

v0:
```python
import functools
import math

import jax
import jax.numpy as jnp
from jax import lax
from jax.experimental import pallas as pl
from jax.experimental.pallas import tpu as pltpu
from jax.sharding import PartitionSpec as P

CEILING = 4.0
MESH = pl.DeviceIdType.MESH


def relay(dims, x, w1, w2, b1_in, b2_in, l1_in, l2_in, o, b1, b2, l1, l2, raw1, far1, raw2, far2, til1, til2, col1, col2,
          in_a, in_b, mid, res, acc, s_w, r_w, l_w, s_in, s_a, r_a, s_f, s_b, r_b, s_o, r_o, ready):
    n, sections, span, chunks, tile = dims
    me = lax.axis_index("owners")
    sec = lax.axis_index("section")
    rep = lax.axis_index("rep")
    piece = x.shape[1]
    width = n * piece
    rows = x.shape[2]
    blocks = width // tile
    half = w1.shape[0]
    per = n // chunks
    sub = blocks // chunks
    last = sections - 1

    barrier = pltpu.get_barrier_semaphore()
    par = lax.rem(me, span)
    base = me - par
    classes = n // span

    def fellow(k):
        return lax.rem(me + span * k, n)

    def mate(j):
        return base + lax.rem(par + j, span)

    def greet(sem, w, t):
        pl.semaphore_signal(sem, inc=1, device_id={"owners": w, "section": t}, device_id_type=MESH)

    near = [fellow(k) for k in range(1, classes)] + [mate(j) for j in range(1, span)]

    @pl.when(sec == 0)
    def _():
        for w in near:
            greet(barrier, w, 0)
    for t in range(1, sections):
        for w in range(n):
            @pl.when(jnp.logical_or(me != w, sec != t))
            def _():
                greet(barrier, w, t)
    pl.semaphore_signal(barrier, inc=1, device_id={"rep": 1 - rep}, device_id_type=MESH)

    local = [
        pltpu.make_async_copy(w1, raw1, l_w.at[0]),
        pltpu.make_async_copy(w2, raw2, l_w.at[1]),
        pltpu.make_async_copy(l1_in, l1, l_w.at[2]),
        pltpu.make_async_copy(l2_in, l2, l_w.at[3]),
        pltpu.make_async_copy(b1_in, b1, l_w.at[4]),
        pltpu.make_async_copy(b2_in, b2, l_w.at[5]),
    ]
    for copy in local:
        copy.start()
    @pl.when(sec == 0)
    def _():
        pl.semaphore_wait(barrier, len(near) + 1)

    @pl.when(sec != 0)
    def _():
        pl.semaphore_wait(barrier, n * sections)

    @pl.when(sec == 1)
    def _():
        for k in range(classes):
            greet(ready, fellow(k), 0)

    bytes_of = in_a.at[0, 0, 0]

    def send_a(src, slot, h, w, target, sem):
        pltpu.make_async_remote_copy(
            src_ref=src.at[(w // span) * span + h], dst_ref=in_a.at[slot, h, me],
            send_sem=sem.at[h, w], recv_sem=r_a.at[slot, h, me],
            device_id={"owners": w, "section": target}, device_id_type=MESH).start()

    def done(sem):
        pltpu.make_async_copy(bytes_of, bytes_of, sem).wait()

    @pl.when(sec == 0)
    def _():
        for w in near:
            for h in range(span):
                send_a(x, 0, h, w, 0, s_in)
        for h in range(span):
            pltpu.make_async_copy(x.at[base + h], in_a.at[0, h, me], r_a.at[0, h, me]).start()

    @pl.when(sec != 0)
    def _():
        for d in range(n - 1, -1, -1):
            for h in range(span):
                send_a(x, sec + 1, h, lax.rem(me + d, n), 0, s_in)

    def weight_copy(src, dst, k):
        return pltpu.make_async_remote_copy(
            src_ref=src, dst_ref=dst,
            send_sem=s_w.at[k], recv_sem=r_w.at[k],
            device_id={"rep": 1 - rep}, device_id_type=MESH)

    weight_copy(w1, far1, 0).start()
    weight_copy(w2, far2, 1).start()

    def arrange(raw, til, links, begin, spans):
        radix = spans * blocks

        def one(b, carry):
            i = b + begin
            taken = [links[i, k] for k in range(radix)]
            for p in range(radix):
                slot = jnp.int32(0)
                for k in range(1, radix):
                    slot = jnp.where(taken[k] == p, k, slot)
                h, j = p // blocks, p % blocks
                c, q = j // sub, h * sub + j % sub
                til[c, pl.ds(pl.multiple_of(i * tile, tile), tile), q * tile:(q + 1) * tile] = raw[b, slot].T
            return carry

        lax.fori_loop(0, half, one, 0)

    def bias_columns(b, col):
        for i in range(blocks):
            row = b[0:1, i * tile:(i + 1) * tile]
            col[i * tile:(i + 1) * tile, :] = jnp.broadcast_to(row, (rows, tile)).T

    for copy in local[2:]:
        copy.wait()
    bias_columns(b1, col1)
    bias_columns(b2, col2)
    local[0].wait()
    arrange(raw1, til1, l1, rep * half, span)
    weight_copy(w1, far1, 0).wait_recv()
    arrange(far1, til1, l1, (1 - rep) * half, span)

    def finish(col):
        return jnp.clip(acc[...] + col[...], 0.0, CEILING).astype(jnp.bfloat16)

    mine = me // per
    order = sorted(range(chunks), key=lambda d: (d % span, d))

    def slot_of(m):
        return jnp.where(sec == 0, 0, 1) if m == 0 else m + 1

    def forward(m, h, u, j):
        slot = slot_of(m)
        return pltpu.make_async_remote_copy(
            src_ref=in_a.at[slot, h, u], dst_ref=in_a.at[slot, h, u],
            send_sem=s_f.at[m, h, u, j - 1], recv_sem=r_a.at[slot, h, u],
            device_id={"owners": mate(j)}, device_id_type=MESH)

    def forwards(m, act):
        for k in range(classes):
            def go():
                for h in range(span):
                    for j in range(1, span):
                        act(forward(m, h, fellow(k), j))
            if m == last:
                if m == 0 and k > 0:
                    pl.when(sec == 0)(go)
            elif m == 0 and k > 0:
                go()
            else:
                pl.when(sec > 0)(go)

    def first_layer(m):
        slot = slot_of(m)
        for k in range(classes):
            u = fellow(k)
            for h in range(span):
                done(r_a.at[slot, h, u])

                def go():
                    for j in range(1, span):
                        forward(m, h, u, j).start()
                if m == last:
                    if m == 0 and k > 0:
                        pl.when(sec == 0)(go)
                elif m == 0 and k > 0:
                    go()
                else:
                    pl.when(sec > 0)(go)
        for e, d in enumerate(order):
            c = lax.rem(mine + d, chunks)
            for k in range(per):
                u = c * per + k

                @pl.when(lax.rem(u, span) != par)
                def _():
                    for h in range(span):
                        done(r_a.at[slot, h, u])
            v = in_a[slot, :, pl.ds(c * per, per)].reshape(span * per * piece, rows)
            part = jnp.dot(til1[c], v, preferred_element_type=jnp.float32)
            acc[...] = part if e == 0 else acc[...] + part
        mid[m] = finish(col1).reshape(n, piece, rows)
        for d in range(n - 1, 0, -1):
            w = lax.rem(me + d, n)
            pltpu.make_async_remote_copy(
                src_ref=mid.at[m, w], dst_ref=in_b.at[m, me],
                send_sem=s_b.at[m, d], recv_sem=r_b.at[m, me],
                device_id={"owners": w}, device_id_type=MESH).start()
        in_b[m, me] = mid[m, me]

    def second_layer(m):
        for d in range(chunks):
            c = lax.rem(mine + d, chunks)
            for k in range(per):
                u = c * per + k
                if d == 0:
                    @pl.when(u != me)
                    def _():
                        done(r_b.at[m, u])
                else:
                    done(r_b.at[m, u])
            v = in_b[m, pl.ds(c * per, per)].reshape(per * piece, rows)
            part = jnp.dot(til2[c], v, preferred_element_type=jnp.float32)
            acc[...] = part if d == 0 else acc[...] + part
        res[m] = finish(col2).reshape(n, piece, rows)

        if last > 0:
            @pl.when(sec < last)
            def _():
                if m == 0:
                    @pl.when(sec == 0)
                    def _():
                        pl.semaphore_wait(ready, classes)
                for d in (range(n - 1, -1, -1) if m == last else range(n - span, -1, -span)):
                    for h in range(span):
                        send_a(res.at[m], m + 1, h, lax.rem(me + d, n), sec + 1, s_a.at[m])

        @pl.when(sec == last)
        def _():
            if m == last:
                o[...] = res[m]
            else:
                pltpu.make_async_remote_copy(
                    src_ref=res.at[m], dst_ref=o, send_sem=s_o.at[m], recv_sem=r_o.at[0],
                    device_id={"section": m}, device_id_type=MESH).start()

    first_layer(0)
    local[1].wait()
    arrange(raw2, til2, l2, rep * half, 1)
    weight_copy(w2, far2, 1).wait_recv()
    arrange(far2, til2, l2, (1 - rep) * half, 1)
    for m in range(sections):
        if m > 0:
            first_layer(m)
        second_layer(m)

    def sent(ref, sem):
        pltpu.make_async_copy(ref, ref, sem).wait()

    @pl.when(sec == 0)
    def _():
        for w in near:
            for h in range(span):
                done(s_in.at[h, w])

    @pl.when(sec != 0)
    def _():
        for w in range(n):
            for h in range(span):
                done(s_in.at[h, w])
    for m in range(sections):
        forwards(m, lambda copy: copy.wait_send())
        for d in range(1, n):
            sent(mid.at[m, 0], s_b.at[m, d])
    weight_copy(w1, far1, 0).wait_send()
    weight_copy(w2, far2, 1).wait_send()
    if last > 0:
        @pl.when(sec < last)
        def _():
            for m in range(sections):
                for d in range(0, n, 1 if m == last else span):
                    for h in range(span):
                        done(s_a.at[m, h, lax.rem(me + d, n)])
            sent(o, r_o.at[0])

        @pl.when(sec == last)
        def _():
            for m in range(last):
                sent(res.at[m], s_o.at[m])


def body(inputs, weight_first, weight_second, bias_first, bias_second, links_first, links_second):
    n = lax.axis_size("owners")
    sections = lax.axis_size("section")
    width, rows = inputs.shape[1:]
    half, deep, tile = weight_first.shape[1:]
    radix_a = links_first.shape[2]
    radix_b = links_second.shape[2]
    blocks = width // tile
    span = radix_a // blocks
    piece = width // n
    chunks = math.gcd(math.gcd(n, blocks), 4)
    dims = (n, sections, span, chunks, tile)
    bf = jnp.bfloat16
    anyspace = pl.BlockSpec(memory_space=pltpu.HBM)
    vmem = pl.BlockSpec(memory_space=pltpu.VMEM)
    dma = pltpu.SemaphoreType.DMA
    out = pl.pallas_call(
        functools.partial(relay, dims),
        name="relay",
        out_shape=jax.ShapeDtypeStruct((n, piece, rows), bf),
        in_specs=[anyspace] * 7,
        out_specs=vmem,
        scratch_shapes=[
            pltpu.VMEM(bias_first.shape, jnp.float32),
            pltpu.VMEM(bias_second.shape, jnp.float32),
            pltpu.SMEM(links_first.shape[1:], jnp.int32),
            pltpu.SMEM(links_second.shape[1:], jnp.int32),
            pltpu.VMEM((half, radix_a, tile, tile), bf),
            pltpu.VMEM((half, radix_a, tile, tile), bf),
            pltpu.VMEM((half, radix_b, tile, tile), bf),
            pltpu.VMEM((half, radix_b, tile, tile), bf),
            pltpu.VMEM((chunks, width, radix_a * tile // chunks), bf),
            pltpu.VMEM((chunks, width, radix_b * tile // chunks), bf),
            pltpu.VMEM((width, rows), jnp.float32),
            pltpu.VMEM((width, rows), jnp.float32),
            pltpu.VMEM((sections + 1, span, n, piece, rows), bf),
            pltpu.VMEM((sections, n, piece, rows), bf),
            pltpu.VMEM((sections, n, piece, rows), bf),
            pltpu.VMEM((sections, n, piece, rows), bf),
            pltpu.VMEM((width, rows), jnp.float32),
            dma((2,)), dma((2,)), dma((6,)),
            dma((span, n)), dma((sections, span, n)), dma((sections + 1, span, n)),
            dma((sections, span, n, max(span - 1, 1))),
            dma((sections, n)), dma((sections, n)),
            dma((sections,)), dma((1,)), pltpu.SemaphoreType.REGULAR,
        ],
        compiler_params=pltpu.CompilerParams(
            collective_id=0, has_side_effects=True, vmem_limit_bytes=67043328),
    )(
        inputs.reshape(n, piece, rows),
        weight_first.reshape(half, radix_a, tile, tile),
        weight_second.reshape(half, radix_b, tile, tile),
        bias_first, bias_second, links_first[0], links_second[0],
    )
    return out.reshape(1, width, rows)


def solution(mesh):
    placed = (
        P("section", "owners", ("groups", "rep")),
        P("section", ("owners", "rep"), None, None),
        P("section", ("owners", "rep"), None, None),
        P("section", "owners"),
        P("section", "owners"),
        P("section", "owners", None),
        P("section", "owners", None),
    )
    return jax.shard_map(
        body,
        mesh=mesh,
        in_specs=placed,
        out_specs=P("section", "owners", ("groups", "rep")),
        check_vma=False,
    )
```

profile of v0, /device:TPU:14, one launch (start us, length us, event | category | flops | bytes accessed | tf_op | source)
XLA Modules:
  0.0 59.0 jit_solution(16131899358090352591)
XLA Ops:
  0.0 57.3 %relay.1 = bf16[4,256,128]{2,1,0:T(8,128)(2,1)} custom-call(bf16[4,256,128]{2,1,0:T(8,128)(2,1)} %bitcast.9, bf16[4,16,128,128]{3,2,1,0:T(8,128)(2,1)} %bitcast.6, bf16[4,8,128,128]{3,2,1,0:T(8,128)(2,1)} %bitcast.8, f32[1,1024]{1,0:T(1,128)} %b1_in.1, f32[1,1024]{1,0:T(1,128)} %b2_in.1, s32[8,16]{1,0:T(8,128)} %bitcast.10, s32[8,8]{1,0:T(8,128)} %bitcast.11), custom_call_target="tpu_custom_call" | custom-call | tf_op jit(solution)/shard_map/relay/pallas_call | solution.py:310
  57.3 1.7 %copy.9 = bf16[1,1024,128]{2,1,0:T(8,128)(2,1)} copy(bf16[1,1024,128]{2,1,0:T(8,128)(2,1)} %bitcast.7) | data formatting | bytes 524288
where the time goes:
time: 59.8 us; the launch traced here: 59 us
  Pallas kernels  57.3 us (96%)
  local copies, waits for them, and re-layouts  1.67 us (3%)
    pallas_call x1, Pallas kernels, body(): pl.pallas_call(functools.partial(relay, dims), name='relay', out_shape=ja...  57.3 us
    unnamed x1, local copies, waits for them, and re-layouts  1.67 us

commit v1 on v0

--- a/solution.py
+++ b/solution.py
@@ -1,5 +1,4 @@
 import functools
-import math
 
 import jax
 import jax.numpy as jnp
@@ -13,8 +12,8 @@
 
 
 def relay(dims, x, w1, w2, b1_in, b2_in, l1_in, l2_in, o, b1, b2, l1, l2, raw1, far1, raw2, far2, til1, til2, col1, col2,
-          in_a, in_b, mid, res, acc, s_w, r_w, l_w, s_in, s_a, r_a, s_f, s_b, r_b, s_o, r_o, ready):
-    n, sections, span, chunks, tile = dims
+          in_a, in_b, mid, res, via, s_w, r_w, l_w, s_in, s_a, r_a, s_f, s_b, r_b, s_o, r_o, s_v, r_v, ready):
+    n, sections, span, tile = dims
     me = lax.axis_index("owners")
     sec = lax.axis_index("section")
     rep = lax.axis_index("rep")
@@ -23,8 +22,6 @@
     rows = x.shape[2]
     blocks = width // tile
     half = w1.shape[0]
-    per = n // chunks
-    sub = blocks // chunks
     last = sections - 1
 
     barrier = pltpu.get_barrier_semaphore()
@@ -88,6 +85,9 @@
     def done(sem):
         pltpu.make_async_copy(bytes_of, bytes_of, sem).wait()
 
+    def done_piece(sem):
+        pltpu.make_async_copy(via.at[0], via.at[0], sem).wait()
+
     @pl.when(sec == 0)
     def _():
         for w in near:
@@ -121,9 +121,7 @@
                 slot = jnp.int32(0)
                 for k in range(1, radix):
                     slot = jnp.where(taken[k] == p, k, slot)
-                h, j = p // blocks, p % blocks
-                c, q = j // sub, h * sub + j % sub
-                til[c, pl.ds(pl.multiple_of(i * tile, tile), tile), q * tile:(q + 1) * tile] = raw[b, slot].T
+                til[pl.ds(pl.multiple_of(i * tile, tile), tile), p * tile:(p + 1) * tile] = raw[b, slot].T
             return carry
 
         lax.fori_loop(0, half, one, 0)
@@ -142,11 +140,21 @@
     weight_copy(w1, far1, 0).wait_recv()
     arrange(far1, til1, l1, (1 - rep) * half, span)
 
-    def finish(col):
-        return jnp.clip(acc[...] + col[...], 0.0, CEILING).astype(jnp.bfloat16)
-
-    mine = me // per
-    order = sorted(range(chunks), key=lambda d: (d % span, d))
+    def slab(ref, w):
+        return ref[pl.ds(pl.multiple_of(w * piece, piece), piece), :]
+
+    def product(til, v, col, w):
+        part = jnp.dot(slab(til, w), v, preferred_element_type=jnp.float32)
+        return jnp.clip(part + slab(col, w), 0.0, CEILING).astype(jnp.bfloat16)
+
+    def far(d):
+        low, high = me, n - 1 - me
+        short = jnp.minimum(low, high)
+        k = n - 1 - d
+        both = (k + 1) // 2
+        away = jnp.where(k <= 2 * short, both, k - short)
+        up = jnp.where(k <= 2 * short, (k % 2) == 0, high > low)
+        return jnp.where(up, me + away, me - away)
 
     def slot_of(m):
         return jnp.where(sec == 0, 0, 1) if m == 0 else m + 1
@@ -158,19 +166,22 @@
             send_sem=s_f.at[m, h, u, j - 1], recv_sem=r_a.at[slot, h, u],
             device_id={"owners": mate(j)}, device_id_type=MESH)
 
+    def relayed(m, k, act):
+        if m == last:
+            if m == 0 and k > 0:
+                pl.when(sec == 0)(act)
+        elif m == 0 and k > 0:
+            act()
+        else:
+            pl.when(sec > 0)(act)
+
     def forwards(m, act):
         for k in range(classes):
             def go():
                 for h in range(span):
                     for j in range(1, span):
                         act(forward(m, h, fellow(k), j))
-            if m == last:
-                if m == 0 and k > 0:
-                    pl.when(sec == 0)(go)
-            elif m == 0 and k > 0:
-                go()
-            else:
-                pl.when(sec > 0)(go)
+            relayed(m, k, go)
 
     def first_layer(m):
         slot = slot_of(m)
@@ -182,57 +193,46 @@
                 def go():
                     for j in range(1, span):
                         forward(m, h, u, j).start()
-                if m == last:
-                    if m == 0 and k > 0:
-                        pl.when(sec == 0)(go)
-                elif m == 0 and k > 0:
-                    go()
+                relayed(m, k, go)
+        for j in range(1, span):
+            for k in range(classes):
+                for h in range(span):
+                    done(r_a.at[slot, h, lax.rem(mate(j) + span * k, n)])
+        v = in_a[slot].reshape(span * width, rows)
+        for d in range(n):
+            w = far(d)
+            mid[m, w] = product(til1, v, col1, w)
+            if d < n - 1:
+                def straight():
+                    pltpu.make_async_remote_copy(
+                        src_ref=mid.at[m, w], dst_ref=in_b.at[m, me],
+                        send_sem=s_b.at[m, d + 1], recv_sem=r_b.at[m, me],
+                        device_id={"owners": w}, device_id_type=MESH).start()
+
+                def detour():
+                    pltpu.make_async_remote_copy(
+                        src_ref=mid.at[m, w], dst_ref=via.at[w],
+                        send_sem=s_b.at[m, d + 1], recv_sem=r_v.at[w],
+                        device_id={"section": 1}, device_id_type=MESH).start()
+
+                if m == 1:
+                    pl.when(sec == 0)(detour)
+                    pl.when(sec > 0)(straight)
                 else:
-                    pl.when(sec > 0)(go)
-        for e, d in enumerate(order):
-            c = lax.rem(mine + d, chunks)
-            for k in range(per):
-                u = c * per + k
-
-                @pl.when(lax.rem(u, span) != par)
-                def _():
-                    for h in range(span):
-                        done(r_a.at[slot, h, u])
-            v = in_a[slot, :, pl.ds(c * per, per)].reshape(span * per * piece, rows)
-            part = jnp.dot(til1[c], v, preferred_element_type=jnp.float32)
-            acc[...] = part if e == 0 else acc[...] + part
-        mid[m] = finish(col1).reshape(n, piece, rows)
-        for d in range(n - 1, 0, -1):
-            w = lax.rem(me + d, n)
-            pltpu.make_async_remote_copy(
-                src_ref=mid.at[m, w], dst_ref=in_b.at[m, me],
-                send_sem=s_b.at[m, d], recv_sem=r_b.at[m, me],
-                device_id={"owners": w}, device_id_type=MESH).start()
-        in_b[m, me] = mid[m, me]
+                    straight()
+            else:
+                in_b[m, me] = mid[m, me]
 
     def second_layer(m):
-        for d in range(chunks):
-            c = lax.rem(mine + d, chunks)
-            for k in range(per):
-                u = c * per + k
-                if d == 0:
-                    @pl.when(u != me)
-                    def _():
-                        done(r_b.at[m, u])
-                else:
-                    done(r_b.at[m, u])
-            v = in_b[m, pl.ds(c * per, per)].reshape(per * piece, rows)
-            part = jnp.dot(til2[c], v, preferred_element_type=jnp.float32)
-            acc[...] = part if d == 0 else acc[...] + part
-        res[m] = finish(col2).reshape(n, piece, rows)
+        for d in range(1, n):
+            done(r_b.at[m, lax.rem(me + d, n)])
+        v = in_b[m].reshape(width, rows)
+        for w in range(n):
+            res[m, w] = product(til2, v, col2, w)
 
         if last > 0:
             @pl.when(sec < last)
             def _():
-                if m == 0:
-                    @pl.when(sec == 0)
-                    def _():
-                        pl.semaphore_wait(ready, classes)
                 for d in (range(n - 1, -1, -1) if m == last else range(n - span, -1, -span)):
                     for h in range(span):
                         send_a(res.at[m], m + 1, h, lax.rem(me + d, n), sec + 1, s_a.at[m])
@@ -246,15 +246,50 @@
                     src_ref=res.at[m], dst_ref=o, send_sem=s_o.at[m], recv_sem=r_o.at[0],
                     device_id={"section": m}, device_id_type=MESH).start()
 
+    def arrange_second():
+        local[1].wait()
+        arrange(raw2, til2, l2, rep * half, 1)
+        weight_copy(w2, far2, 1).wait_recv()
+        arrange(far2, til2, l2, (1 - rep) * half, 1)
+
+    def onward(w):
+        return pltpu.make_async_remote_copy(
+            src_ref=via.at[w], dst_ref=in_b.at[1, me], send_sem=s_v.at[w], recv_sem=r_b.at[1, me],
+            device_id={"owners": w, "section": 0}, device_id_type=MESH)
+
+    @pl.when(sec > 0)
+    def _():
+        arrange_second()
+
+    if last > 0:
+        @pl.when(sec == 1)
+        def _():
+            for d in range(n - 1):
+                w = far(d)
+                done_piece(r_v.at[w])
+                onward(w).start()
+
     first_layer(0)
-    local[1].wait()
-    arrange(raw2, til2, l2, rep * half, 1)
-    weight_copy(w2, far2, 1).wait_recv()
-    arrange(far2, til2, l2, (1 - rep) * half, 1)
+
+    @pl.when(sec == 0)
+    def _():
+        arrange_second()
+
+    if last > 0:
+        @pl.when(sec == 0)
+        def _():
+            pl.semaphore_wait(ready, classes)
+
     for m in range(sections):
-        if m > 0:
-            first_layer(m)
+        if m < last:
+            @pl.when(sec == 0)
+            def _():
+                first_layer(m + 1)
         second_layer(m)
+        if m < last:
+            @pl.when(sec > 0)
+            def _():
+                first_layer(m + 1)
 
     def sent(ref, sem):
         pltpu.make_async_copy(ref, ref, sem).wait()
@@ -277,6 +312,11 @@
     weight_copy(w1, far1, 0).wait_send()
     weight_copy(w2, far2, 1).wait_send()
     if last > 0:
+        @pl.when(sec == 1)
+        def _():
+            for d in range(n - 1):
+                onward(far(d)).wait_send()
+
         @pl.when(sec < last)
         def _():
             for m in range(sections):
@@ -301,8 +341,7 @@
     blocks = width // tile
     span = radix_a // blocks
     piece = width // n
-    chunks = math.gcd(math.gcd(n, blocks), 4)
-    dims = (n, sections, span, chunks, tile)
+    dims = (n, sections, span, tile)
     bf = jnp.bfloat16
     anyspace = pl.BlockSpec(memory_space=pltpu.HBM)
     vmem = pl.BlockSpec(memory_space=pltpu.VMEM)
@@ -322,20 +361,20 @@
             pltpu.VMEM((half, radix_a, tile, tile), bf),
             pltpu.VMEM((half, radix_b, tile, tile), bf),
             pltpu.VMEM((half, radix_b, tile, tile), bf),
-            pltpu.VMEM((chunks, width, radix_a * tile // chunks), bf),
-            pltpu.VMEM((chunks, width, radix_b * tile // chunks), bf),
+            pltpu.VMEM((width, radix_a * tile), bf),
+            pltpu.VMEM((width, radix_b * tile), bf),
             pltpu.VMEM((width, rows), jnp.float32),
             pltpu.VMEM((width, rows), jnp.float32),
             pltpu.VMEM((sections + 1, span, n, piece, rows), bf),
             pltpu.VMEM((sections, n, piece, rows), bf),
             pltpu.VMEM((sections, n, piece, rows), bf),
             pltpu.VMEM((sections, n, piece, rows), bf),
-            pltpu.VMEM((width, rows), jnp.float32),
+            pltpu.VMEM((n, piece, rows), bf),
             dma((2,)), dma((2,)), dma((6,)),
             dma((span, n)), dma((sections, span, n)), dma((sections + 1, span, n)),
             dma((sections, span, n, max(span - 1, 1))),
             dma((sections, n)), dma((sections, n)),
-            dma((sections,)), dma((1,)), pltpu.SemaphoreType.REGULAR,
+            dma((sections,)), dma((1,)), dma((n,)), dma((n,)), pltpu.SemaphoreType.REGULAR,
         ],
         compiler_params=pltpu.CompilerParams(
             collective_id=0, has_side_effects=True, vmem_limit_bytes=67043328),

time: 59.8 us -> 55.9 us (0.935)
  Pallas kernels: 57.3 us -> 53.5 us
    pallas_call x1, Pallas kernels: 57.3 us -> 53.5 us  [body(): pl.pallas_call(functools.partial(relay, dims), name='relay', out_shape=ja...]
where the time goes in v1:
time: 55.9 us; the launch traced here: 55.1 us
  Pallas kernels  53.5 us (96%)
  local copies, waits for them, and re-layouts  1.67 us (3%)
    pallas_call x1, Pallas kernels, body(): pl.pallas_call(functools.partial(relay, dims), name='relay', out_shape=ja...  53.5 us
    unnamed x1, local copies, waits for them, and re-layouts  1.67 us

profile of v1, /device:TPU:14, one launch (start us, length us, event | category | flops | bytes accessed | tf_op | source)
XLA Modules:
  0.0 55.1 jit_solution(7329303416516569099)
XLA Ops:
  0.0 53.5 %relay.1 = bf16[4,256,128]{2,1,0:T(8,128)(2,1)} custom-call(bf16[4,256,128]{2,1,0:T(8,128)(2,1)} %bitcast.9, bf16[4,16,128,128]{3,2,1,0:T(8,128)(2,1)} %bitcast.6, bf16[4,8,128,128]{3,2,1,0:T(8,128)(2,1)} %bitcast.8, f32[1,1024]{1,0:T(1,128)} %b1_in.1, f32[1,1024]{1,0:T(1,128)} %b2_in.1, s32[8,16]{1,0:T(8,128)} %bitcast.10, s32[8,8]{1,0:T(8,128)} %bitcast.11), custom_call_target="tpu_custom_call" | custom-call | tf_op jit(solution)/shard_map/relay/pallas_call | solution.py:349
  53.5 1.7 %copy.9 = bf16[1,1024,128]{2,1,0:T(8,128)(2,1)} copy(bf16[1,1024,128]{2,1,0:T(8,128)(2,1)} %bitcast.7) | data formatting | bytes 524288

commit v2 on v1

--- a/solution.py
+++ b/solution.py
@@ -185,15 +185,24 @@
 
     def first_layer(m):
         slot = slot_of(m)
-        for k in range(classes):
-            u = fellow(k)
+        def pull(u, passing):
             for h in range(span):
                 done(r_a.at[slot, h, u])
-
-                def go():
+                if passing:
                     for j in range(1, span):
                         forward(m, h, u, j).start()
-                relayed(m, k, go)
+
+        @pl.when(sec == 0)
+        def _():
+            for k in range(classes):
+                pull(fellow(k), m == 0 and k > 0)
+
+        @pl.when(sec > 0)
+        def _():
+            edge = jnp.logical_or(me == 0, me == n - 1)
+            for k in range(classes):
+                pull(fellow(jnp.where(edge, k, classes - 1 - k)), m < last)
+
         for j in range(1, span):
             for k in range(classes):
                 for h in range(span):
@@ -223,28 +232,38 @@
             else:
                 in_b[m, me] = mid[m, me]
 
+    def home(m, first):
+        part = pl.ds(first, span)
+        return pltpu.make_async_remote_copy(
+            src_ref=res.at[m, part], dst_ref=o.at[part], send_sem=s_o.at[m, first // span], recv_sem=r_o.at[first // span],
+            device_id={"section": m}, device_id_type=MESH)
+
     def second_layer(m):
         for d in range(1, n):
             done(r_b.at[m, lax.rem(me + d, n)])
         v = in_b[m].reshape(width, rows)
-        for w in range(n):
-            res[m, w] = product(til2, v, col2, w)
-
-        if last > 0:
-            @pl.when(sec < last)
-            def _():
-                for d in (range(n - 1, -1, -1) if m == last else range(n - span, -1, -span)):
-                    for h in range(span):
-                        send_a(res.at[m], m + 1, h, lax.rem(me + d, n), sec + 1, s_a.at[m])
-
-        @pl.when(sec == last)
-        def _():
-            if m == last:
-                o[...] = res[m]
-            else:
-                pltpu.make_async_remote_copy(
-                    src_ref=res.at[m], dst_ref=o, send_sem=s_o.at[m], recv_sem=r_o.at[0],
-                    device_id={"section": m}, device_id_type=MESH).start()
+        for d in range(n - span, -1, -span):
+            w = lax.rem(me + d, n)
+            first = w - lax.rem(w, span)
+            for h in range(span):
+                value = product(til2, v, col2, first + h)
+                res[m, first + h] = value
+                if m == last:
+                    @pl.when(sec == last)
+                    def _():
+                        o[first + h] = value
+
+            if last > 0:
+                @pl.when(sec < last)
+                def _():
+                    for j in range(span if m == last else 1):
+                        for h in range(span):
+                            send_a(res.at[m], m + 1, h, first + lax.rem(w - first + j, span), sec + 1, s_a.at[m])
+
+            if m < last:
+                @pl.when(sec == last)
+                def _():
+                    home(m, first).start()
 
     def arrange_second():
         local[1].wait()
@@ -271,10 +290,6 @@
 
     first_layer(0)
 
-    @pl.when(sec == 0)
-    def _():
-        arrange_second()
-
     if last > 0:
         @pl.when(sec == 0)
         def _():
@@ -285,6 +300,10 @@
             @pl.when(sec == 0)
             def _():
                 first_layer(m + 1)
+        if m == 0:
+            @pl.when(sec == 0)
+            def _():
+                arrange_second()
         second_layer(m)
         if m < last:
             @pl.when(sec > 0)
@@ -323,12 +342,14 @@
                 for d in range(0, n, 1 if m == last else span):
                     for h in range(span):
                         done(s_a.at[m, h, lax.rem(me + d, n)])
-            sent(o, r_o.at[0])
+            for k in range(classes):
+                sent(o.at[pl.ds(0, span)], r_o.at[k])
 
         @pl.when(sec == last)
         def _():
             for m in range(last):
-                sent(res.at[m], s_o.at[m])
+                for k in range(classes):
+                    home(m, k * span).wait_send()
 
 
 def body(inputs, weight_first, weight_second, bias_first, bias_second, links_first, links_second):
@@ -349,7 +370,7 @@
     out = pl.pallas_call(
         functools.partial(relay, dims),
         name="relay",
-        out_shape=jax.ShapeDtypeStruct((n, piece, rows), bf),
+        out_shape=pltpu.VMEM((n, piece, rows), bf),
         in_specs=[anyspace] * 7,
         out_specs=vmem,
         scratch_shapes=[
@@ -374,10 +395,10 @@
             dma((span, n)), dma((sections, span, n)), dma((sections + 1, span, n)),
             dma((sections, span, n, max(span - 1, 1))),
             dma((sections, n)), dma((sections, n)),
-            dma((sections,)), dma((1,)), dma((n,)), dma((n,)), pltpu.SemaphoreType.REGULAR,
+            dma((sections, n // span)), dma((n // span,)), dma((n,)), dma((n,)), pltpu.SemaphoreType.REGULAR,
         ],
         compiler_params=pltpu.CompilerParams(
-            collective_id=0, has_side_effects=True, vmem_limit_bytes=67043328),
+            collective_id=0, has_side_effects=True, vmem_limit_bytes=63 * 2 ** 20 + 2 ** 19),
     )(
         inputs.reshape(n, piece, rows),
         weight_first.reshape(half, radix_a, tile, tile),

time: 55.9 us -> 51.9 us (0.928)
  Pallas kernels: 53.5 us -> 50.9 us
  local copies, waits for them, and re-layouts: 1.67 us -> 0.71 us
    pallas_call x1, Pallas kernels: 53.5 us -> 50.9 us  [body(): pl.pallas_call(functools.partial(relay, dims), name='relay', out_shape=pl...]
    unnamed x1, local copies, waits for them, and re-layouts: 1.67 us -> 0.71 us
where the time goes in v2:
time: 51.9 us; the launch traced here: 51.6 us
  Pallas kernels  50.9 us (98%)
  local copies, waits for them, and re-layouts  0.71 us (1%)
    pallas_call x1, Pallas kernels, body(): pl.pallas_call(functools.partial(relay, dims), name='relay', out_shape=pl...  50.9 us

profile of v2, /device:TPU:14, one launch (start us, length us, event | category | flops | bytes accessed | tf_op | source)
XLA Modules:
  0.0 51.6 jit_solution(8540351760294947744)
XLA Ops:
  0.0 50.9 %relay.1 = bf16[4,256,128]{2,1,0:T(8,128)(2,1)S(1)} custom-call(bf16[4,256,128]{2,1,0:T(8,128)(2,1)} %bitcast.9, bf16[4,16,128,128]{3,2,1,0:T(8,128)(2,1)} %bitcast.7, bf16[4,8,128,128]{3,2,1,0:T(8,128)(2,1)} %bitcast.8, f32[1,1024]{1,0:T(1,128)} %b1_in.1, f32[1,1024]{1,0:T(1,128)} %b2_in.1, s32[8,16]{1,0:T(8,128)} %bitcast.10, s32[8,8]{1,0:T(8,128)} %bitcast.11), custom_call_target="tpu_custom_call" | custom-call | tf_op jit(solution)/shard_map/relay/pallas_call | solution.py:370
  50.9 0.7 %copy.9 = bf16[1,1024,128]{2,1,0:T(8,128)(2,1)} copy(bf16[1,1024,128]{2,1,0:T(8,128)(2,1)S(1)} %bitcast.6) | data formatting | bytes 524288

commit v3 on v2

--- a/solution.py
+++ b/solution.py
@@ -200,7 +200,15 @@
         @pl.when(sec > 0)
         def _():
             edge = jnp.logical_or(me == 0, me == n - 1)
+            if m == 0:
+                @pl.when(jnp.logical_and(sec == 1, edge))
+                def _():
+                    pass_on(True)
             for k in range(classes):
+                if m == 0 and k == classes - 1:
+                    @pl.when(jnp.logical_and(sec == 1, jnp.logical_not(edge)))
+                    def _():
+                        pass_on(True)
                 pull(fellow(jnp.where(edge, k, classes - 1 - k)), m < last)
 
         for j in range(1, span):
@@ -280,13 +288,22 @@
     def _():
         arrange_second()
 
+    def apart(w):
+        return jnp.logical_or(w < base, w >= base + span)
+
+    def pass_on(near_ones):
+        for d in range(n - 1):
+            w = far(d)
+
+            @pl.when(jnp.logical_xor(apart(w), near_ones))
+            def _():
+                done_piece(r_v.at[w])
+                onward(w).start()
+
     if last > 0:
         @pl.when(sec == 1)
         def _():
-            for d in range(n - 1):
-                w = far(d)
-                done_piece(r_v.at[w])
-                onward(w).start()
+            pass_on(False)
 
     first_layer(0)
 

time: 51.9 us -> 50.6 us (0.975)
  Pallas kernels: 50.9 us -> 49.8 us
    pallas_call x1, Pallas kernels: 50.9 us -> 49.8 us  [body(): pl.pallas_call(functools.partial(relay, dims), name='relay', out_shape=pl...]
where the time goes in v3:
time: 50.6 us; the launch traced here: 50.5 us
  Pallas kernels  49.8 us (98%)
  local copies, waits for them, and re-layouts  0.71 us (1%)
    pallas_call x1, Pallas kernels, body(): pl.pallas_call(functools.partial(relay, dims), name='relay', out_shape=pl...  49.8 us

profile of v3, /device:TPU:14, one launch (start us, length us, event | category | flops | bytes accessed | tf_op | source)
XLA Modules:
  0.0 50.5 jit_solution(16795626860380296423)
XLA Ops:
  0.0 49.8 %relay.1 = bf16[4,256,128]{2,1,0:T(8,128)(2,1)S(1)} custom-call(bf16[4,256,128]{2,1,0:T(8,128)(2,1)} %bitcast.9, bf16[4,16,128,128]{3,2,1,0:T(8,128)(2,1)} %bitcast.7, bf16[4,8,128,128]{3,2,1,0:T(8,128)(2,1)} %bitcast.8, f32[1,1024]{1,0:T(1,128)} %b1_in.1, f32[1,1024]{1,0:T(1,128)} %b2_in.1, s32[8,16]{1,0:T(8,128)} %bitcast.10, s32[8,8]{1,0:T(8,128)} %bitcast.11), custom_call_target="tpu_custom_call" | custom-call | tf_op jit(solution)/shard_map/relay/pallas_call | solution.py:387
  49.8 0.7 %copy.9 = bf16[1,1024,128]{2,1,0:T(8,128)(2,1)} copy(bf16[1,1024,128]{2,1,0:T(8,128)(2,1)S(1)} %bitcast.6) | data formatting | bytes 524288

commit v4 on v3

--- a/solution.py
+++ b/solution.py
@@ -12,7 +12,7 @@
 
 
 def relay(dims, x, w1, w2, b1_in, b2_in, l1_in, l2_in, o, b1, b2, l1, l2, raw1, far1, raw2, far2, til1, til2, col1, col2,
-          in_a, in_b, mid, res, via, s_w, r_w, l_w, s_in, s_a, r_a, s_f, s_b, r_b, s_o, r_o, s_v, r_v, ready):
+          in_a, in_b, mid, res, via, acc, s_w, r_w, l_w, s_in, s_a, r_a, s_f, s_b, r_b, s_o, r_o, s_v, r_v, ready):
     n, sections, span, tile = dims
     me = lax.axis_index("owners")
     sec = lax.axis_index("section")
@@ -143,9 +143,23 @@
     def slab(ref, w):
         return ref[pl.ds(pl.multiple_of(w * piece, piece), piece), :]
 
-    def product(til, v, col, w):
-        part = jnp.dot(slab(til, w), v, preferred_element_type=jnp.float32)
+    def bounds(part, col, w):
         return jnp.clip(part + slab(col, w), 0.0, CEILING).astype(jnp.bfloat16)
+
+    def columns(til, height, u, spans):
+        return jnp.concatenate(
+            [til[height, pl.ds(pl.multiple_of(h * width + u * piece, tile), piece)] for h in range(spans)], axis=1)
+
+    def gather_up(til, u, v, spans, fresh):
+        part = jnp.dot(columns(til, slice(None), u, spans), v, preferred_element_type=jnp.float32)
+        acc[...] = part if fresh else acc[...] + part
+
+    def product(til, v, col, w, u, spans):
+        if u is None:
+            return bounds(jnp.dot(slab(til, w), v, preferred_element_type=jnp.float32), col, w)
+        height = pl.ds(pl.multiple_of(w * piece, piece), piece)
+        part = jnp.dot(columns(til, height, u, spans), v, preferred_element_type=jnp.float32)
+        return bounds(slab(acc, w) + part, col, w)
 
     def far(d):
         low, high = me, n - 1 - me
@@ -156,6 +170,12 @@
         up = jnp.where(k <= 2 * short, (k % 2) == 0, high > low)
         return jnp.where(up, me + away, me - away)
 
+    def detour_order(d):
+        other = mate(1) if span > 1 else far(0)
+        at = sum(jnp.where(far(i) == other, i, 0) for i in range(n))
+        w = other if d == 0 else jnp.where(d - 1 < at, far(d - 1), far(d))
+        return jnp.where(sec == 0, w, far(d))
+
     def slot_of(m):
         return jnp.where(sec == 0, 0, 1) if m == 0 else m + 1
 
@@ -200,25 +220,33 @@
         @pl.when(sec > 0)
         def _():
             edge = jnp.logical_or(me == 0, me == n - 1)
-            if m == 0:
-                @pl.when(jnp.logical_and(sec == 1, edge))
-                def _():
-                    pass_on(True)
             for k in range(classes):
-                if m == 0 and k == classes - 1:
-                    @pl.when(jnp.logical_and(sec == 1, jnp.logical_not(edge)))
-                    def _():
-                        pass_on(True)
                 pull(fellow(jnp.where(edge, k, classes - 1 - k)), m < last)
 
-        for j in range(1, span):
-            for k in range(classes):
-                for h in range(span):
-                    done(r_a.at[slot, h, lax.rem(mate(j) + span * k, n)])
-        v = in_a[slot].reshape(span * width, rows)
+        turned = jnp.logical_and(sec > 0, jnp.logical_or(me == 0, me == n - 1))
+        others = [
+            lax.rem(mate(j) + span * (jnp.where(turned, classes - 1 - k, k) if m == 0 else k), n)
+            for j in range(1, span) for k in range(classes)]
+        sources = [fellow(k) for k in range(classes)] + others
+
+        def landed(u):
+            for h in range(span):
+                done(r_a.at[slot, h, u])
+
+        if piece % tile == 0 and n > 1 and m == 0:
+            for i, u in enumerate(sources):
+                if i >= classes:
+                    landed(u)
+                v = jnp.concatenate([in_a[slot, h, u] for h in range(span)], axis=0)
+                if i < n - 1:
+                    gather_up(til1, u, v, span, i == 0)
+        else:
+            for u in others:
+                landed(u)
+            u, v = None, in_a[slot].reshape(span * width, rows)
         for d in range(n):
-            w = far(d)
-            mid[m, w] = product(til1, v, col1, w)
+            w = detour_order(d) if m == 1 else far(d)
+            mid[m, w] = product(til1, v, col1, w, u, span)
             if d < n - 1:
                 def straight():
                     pltpu.make_async_remote_copy(
@@ -247,14 +275,23 @@
             device_id={"section": m}, device_id_type=MESH)
 
     def second_layer(m):
-        for d in range(1, n):
-            done(r_b.at[m, lax.rem(me + d, n)])
-        v = in_b[m].reshape(width, rows)
+        if piece % tile == 0 and n > 1 and False:
+            for i in range(n):
+                u = far(n - 1 - i)
+                if i > 0:
+                    done(r_b.at[m, u])
+                v = in_b[m, u]
+                if i < n - 1:
+                    gather_up(til2, u, v, 1, i == 0)
+        else:
+            for d in range(1, n):
+                done(r_b.at[m, lax.rem(me + d, n)])
+            u, v = None, in_b[m].reshape(width, rows)
         for d in range(n - span, -1, -span):
             w = lax.rem(me + d, n)
             first = w - lax.rem(w, span)
             for h in range(span):
-                value = product(til2, v, col2, first + h)
+                value = product(til2, v, col2, first + h, u, 1)
                 res[m, first + h] = value
                 if m == last:
                     @pl.when(sec == last)
@@ -303,6 +340,7 @@
     if last > 0:
         @pl.when(sec == 1)
         def _():
+            pass_on(True)
             pass_on(False)
 
     first_layer(0)
@@ -408,6 +446,7 @@
             pltpu.VMEM((sections, n, piece, rows), bf),
             pltpu.VMEM((sections, n, piece, rows), bf),
             pltpu.VMEM((n, piece, rows), bf),
+            pltpu.VMEM((width, rows), jnp.float32),
             dma((2,)), dma((2,)), dma((6,)),
             dma((span, n)), dma((sections, span, n)), dma((sections + 1, span, n)),
             dma((sections, span, n, max(span - 1, 1))),

time: 50.6 us -> 49.1 us (0.970); the launches traced: 50.5 us -> 48.5 us
  Pallas kernels: 49.8 us -> 47.8 us
    pallas_call x1, Pallas kernels: 49.8 us -> 47.8 us  [body(): pl.pallas_call(functools.partial(relay, dims), name='relay', out_shape=pl...]
where the time goes in v4:
time: 49.1 us; the launch traced here: 48.5 us
  Pallas kernels  47.8 us (97%)
  local copies, waits for them, and re-layouts  0.71 us (1%)
    pallas_call x1, Pallas kernels, body(): pl.pallas_call(functools.partial(relay, dims), name='relay', out_shape=pl...  47.8 us

profile of v4, /device:TPU:14, one launch (start us, length us, event | category | flops | bytes accessed | tf_op | source)
XLA Modules:
  0.0 48.5 jit_solution(11274875098639410924)
XLA Ops:
  0.0 47.8 %relay.1 = bf16[4,256,128]{2,1,0:T(8,128)(2,1)S(1)} custom-call(bf16[4,256,128]{2,1,0:T(8,128)(2,1)} %bitcast.9, bf16[4,16,128,128]{3,2,1,0:T(8,128)(2,1)} %bitcast.7, bf16[4,8,128,128]{3,2,1,0:T(8,128)(2,1)} %bitcast.8, f32[1,1024]{1,0:T(1,128)} %b1_in.1, f32[1,1024]{1,0:T(1,128)} %b2_in.1, s32[8,16]{1,0:T(8,128)} %bitcast.10, s32[8,8]{1,0:T(8,128)} %bitcast.11), custom_call_target="tpu_custom_call" | custom-call | tf_op jit(solution)/shard_map/relay/pallas_call | solution.py:425
  47.8 0.7 %copy.9 = bf16[1,1024,128]{2,1,0:T(8,128)(2,1)} copy(bf16[1,1024,128]{2,1,0:T(8,128)(2,1)S(1)} %bitcast.6) | data formatting | bytes 524288
